TPU v7x, 32 devices: a whole 2x2x4 slice. The times are simulated.
32 devices in a mesh: groups: 2 (over y), space: 4 (over z), clus: 4 (over x, core).
Axes of the slice: x: 2, y: 2, z: 4, core: 2. Of those that a mesh axis runs over, the one named last changes fastest.
Arguments:
- snapshots: bfloat16 [256, 5, 49152], P('groups', None, ('space', 'clus')), parts along dimension 0
- labels: int32 [256], P('groups'), parts along dimension 0, may hold values from 0 to 3, as said below
- start: float32 [256, 16], P('groups'), parts along dimension 0, may hold values from -6 to 6
- successor: int32 [8], P('groups'), parts along dimension 0, may hold values from 0 to 3, as said below
Outputs:
- modes: bfloat16 [8, 16, 5, 49152], P(('groups', 'clus'), None, None, 'space'), parts along dimension 0
- coefficients: float32 [256, 16], P(('groups', 'clus')), parts along dimension 0
- correlations: float32 [8, 16, 16], P(('groups', 'clus')), parts along dimension 0
There are 2 independent parts, one for each index of `groups`. A program takes and returns all parts, laid end to end along the dimension named above; each array names one. Nothing has to cross between parts.
Inputs may be any that keep to these rules, and one draw needn't show every extreme that they name: `labels`: of the 32 snapshots of each aligned block (those of one index of clus), every cluster holds at least 6 and at most 8; in every block some cluster holds exactly 8. Following successor from any cluster visits all 4 clusters once before returning.
All inputs are finite; a program needn't handle non-finite values.
Results may differ from a plain program's by a relative error of at most 0.0045.
Values may be sent and summed in bfloat16 or wider, within the bound.
No kernel may reach another device: no remote copies, remote signals or barrier semaphores. Data moves between devices by JAX's collectives and lax.ppermute only.
A program may use at most 64 MiB of HBM per device.

v0:
```python
import jax
import jax.numpy as jnp
from jax import lax
from jax.sharding import PartitionSpec as P

ITERS = 2


def subspace(gram, member, start):
    basis = member[:, :, None] * start[None, :, :]
    for step in range(ITERS):
        image = (
            member[:, :, None]
            * jnp.einsum("st,ktm->ksm", gram, basis, precision=lax.Precision.HIGHEST)
            + basis
        )
        inner = jnp.einsum("ksm,ksn->kmn", image, image, precision=lax.Precision.HIGHEST)
        lower = jnp.linalg.cholesky(inner)
        basis = lax.linalg.triangular_solve(
            lower, image, left_side=False, lower=True, transpose_a=True
        )
    return basis


def local(snapshots, labels, start, successor):
    count, variables, cells = snapshots.shape
    clusters = lax.axis_size("clus")
    owner = lax.axis_index("clus")
    total_rows = variables * cells * lax.axis_size("space") * clusters
    flat = snapshots.reshape(count, variables * cells)
    partial_value = lax.dot_general(
        flat, flat, (((1,), (1,)), ((), ())), preferred_element_type=jnp.float32
    )
    gram = lax.psum(partial_value, ("space", "clus")) / total_rows
    cluster_ids = jnp.arange(clusters, dtype=jnp.int32)
    member = (labels[None, :] == cluster_ids[:, None]).astype(jnp.float32)
    basis = subspace(gram, member, start)
    picked = jnp.einsum("ks,ksm->sm", member, basis, precision=lax.Precision.HIGHEST)
    snap_dev = count // clusters
    coefficients = lax.dynamic_slice_in_dim(picked, owner * snap_dev, snap_dev, 0)
    rounded = basis.astype(jnp.bfloat16)
    mode_count = rounded.shape[2]
    modes_full = None
    left = jnp.transpose(rounded, (0, 2, 1)).reshape(clusters * mode_count, count)
    modes_full = jnp.dot(left, flat, preferred_element_type=jnp.float32)
    packed = modes_full.astype(jnp.bfloat16).reshape(clusters, mode_count, variables, cells)
    modes_out = lax.all_to_all(packed, "clus", split_axis=0, concat_axis=3, tiled=True)
    select = (successor[:, None] == cluster_ids[None, :]).astype(jnp.float32)
    wide = rounded.astype(jnp.float32)
    partner = jnp.einsum("ab,bsn->asn", select, wide, precision=lax.Precision.HIGHEST)
    image = jnp.einsum("st,atn->asn", gram, partner, precision=lax.Precision.HIGHEST)
    correlations = jnp.einsum("asm,asn->amn", wide, image, precision=lax.Precision.HIGHEST)
    own_correlation = lax.dynamic_slice_in_dim(correlations, owner, 1, 0)
    return (modes_out, coefficients, own_correlation)


def solution(mesh):
    in_specs = (P("groups", None, ("space", "clus")), P("groups"), P("groups", None), P("groups"))
    out_specs = (
        P(("groups", "clus"), None, None, "space"),
        P(("groups", "clus"), None),
        P(("groups", "clus"), None, None),
    )
    return jax.shard_map(local, mesh=mesh, in_specs=in_specs, out_specs=out_specs, check_vma=False)
```

profile of v0, /device:TPU:8, one launch (start us, length us, event | category | flops | bytes accessed | tf_op | source)
XLA Modules:
  0.0 174.2 jit_solution(173776694287602055)
XLA Ops:
  7.2 5.1 %convolution_bitcast_fusion = f32[128,128]{1,0:T(8,128)} fusion(bf16[128,5,3072]{2,0,1:T(8,128)(2,1)} %param.7), kind=kOutput, calls=%fused_computation.1 | convolution fusion | flops 503316480 | bytes 3997696 | tf_op jit(solution)/shard_map/dot_general | solution.py:31
  12.4 6.3 %copy.38 = bf16[128,5,3072]{0,2,1:T(8,128)(2,1)} copy(bf16[128,5,3072]{2,0,1:T(8,128)(2,1)} %param.7) | data formatting | bytes 7864320 | tf_op args[0]
  18.7 82.0 %all-reduce.2.cloned.1.call-done = f32[128,128]{1,0:T(8,128)} async-done(((f32[128,128]{1,0:T(8,128)}), f32[128,128]{1,0:T(8,128)}) %all-reduce.2.cloned.1.call-update) | async-done | bytes 65552 | tf_op jit(solution)/shard_map/psum | solution.py:34
  100.7 1.1 fusion.3
  101.8 0.2 fusion.35
  102.1 5.9 %custom-call.8 = f32[4,16,16]{2,1,0:T(8,128)S(1)} custom-call(f32[4,16,16]{2,1,0:T(8,128)S(1)} %fusion.16), custom_call_target="Cholesky" | custom-call | tf_op jit(solution)/shard_map/jit(cholesky)/cholesky | solution.py:18
  108.2 4.9 %custom-call.9 = f32[4,1,16,16]{2,3,1,0:T(8,128)S(1)} custom-call(f32[4,1,16,16]{3,2,1,0:T(8,128)S(1)} %select_bitcast_fusion.1), custom_call_target="InvertDiagBlocksLowerTriangular" | custom-call | tf_op jit(solution)/shard_map/triangular_solve/custom-call.0 | solution.py:19
  113.1 0.3 convolution_bitcast_fusion.1
  113.4 1.1 fusion.1
  114.5 0.2 fusion.36
  114.7 5.9 %custom-call.10 = f32[4,16,16]{2,1,0:T(8,128)S(1)} custom-call(f32[4,16,16]{2,1,0:T(8,128)S(1)} %fusion.14), custom_call_target="Cholesky" | custom-call | tf_op jit(solution)/shard_map/jit(cholesky)/cholesky | solution.py:18
  120.8 4.9 %custom-call.11 = f32[4,1,16,16]{2,3,1,0:T(8,128)S(1)} custom-call(f32[4,1,16,16]{3,2,1,0:T(8,128)S(1)} %select_bitcast_fusion), custom_call_target="InvertDiagBlocksLowerTriangular" | custom-call | tf_op jit(solution)/shard_map/triangular_solve/custom-call.0 | solution.py:19
  125.7 0.3 bitcast_convert_fusion
  126.0 4.9 %convolution_convert_fusion = bf16[64,15360]{1,0:T(8,128)(2,1)} fusion(bf16[64,128]{1,0:T(8,128)(2,1)S(1)} %bitcast.78, bf16[128,15360]{0,1:T(8,128)(2,1)} %bitcast.75), kind=kOutput, calls=%fused_computation | convolution fusion | flops 252641280 | bytes 5914624 | tf_op jit(solution)/shard_map/dot_general | solution.py:45
  130.9 4.6 %reshape.50 = bf16[4,16,5,3072]{3,2,1,0:T(8,128)(2,1)S(1)} reshape(bf16[64,15360]{1,0:T(8,128)(2,1)} %convolution_convert_fusion) | data formatting | bytes 3932160 | tf_op jit(solution)/shard_map/reshape | solution.py:46
  135.5 2.6 %copy.39 = bf16[4,16,5,3072]{3,1,2,0:T(8,128)(2,1)} copy(bf16[4,16,5,3072]{3,2,1,0:T(8,128)(2,1)S(1)} %reshape.50) | data formatting | bytes 3932160 | tf_op jit(solution)/shard_map/reshape | solution.py:46
  138.1 3.6 %all-to-all-start = ((bf16[4,16,5,3072]{3,1,2,0:T(8,128)(2,1)}), bf16[4,16,5,3072]{3,1,2,0:T(8,128)(2,1)S(1)}, u32[]{:S(2)}, u32[]{:S(2)}) async-start(bf16[4,16,5,3072]{3,1,2,0:T(8,128)(2,1)} %copy.39), calls=%async_computation | async-start | bytes 3932160 | tf_op jit(solution)/shard_map/all_to_all | solution.py:47
  141.7 0.7 constant_dynamic-slice_fusion.1
  142.4 0.2 fusion.22
  142.6 0.2 fusion.4
  142.8 0.1 fusion.37
  143.0 0.6 constant_dynamic-slice_fusion
  143.6 22.4 %all-to-all-done = bf16[4,16,5,3072]{3,1,2,0:T(8,128)(2,1)S(1)} async-done(((bf16[4,16,5,3072]{3,1,2,0:T(8,128)(2,1)}), bf16[4,16,5,3072]{3,1,2,0:T(8,128)(2,1)S(1)}, u32[]{:S(2)}, u32[]{:S(2)}) %all-to-all-start) | async-done | bytes 1966112 | tf_op jit(solution)/shard_map/all_to_all | solution.py:47
  165.9 1.4 copy.52
  (24 shorter events, 0.7 us)
Async XLA Ops:
  7.2 5.2 %copy-start.2 = (s32[128]{0:T(128)S(1)}, s32[128]{0:T(128)}, u32[]{:S(2)}) copy-start(s32[128]{0:T(128)} %param.8) | copy-start | bytes 1540
  7.2 93.5 %all-reduce.2.cloned.1.call-start = ((), (), s32[]{:S(2)}) async-start(), calls=%async_computation.1 | async-start | bytes 131072 | tf_op jit(solution)/shard_map/psum | solution.py:34
  12.4 88.3 %copy-start.1 = (f32[128,16]{0,1:T(8,128)S(1)}, f32[128,16]{0,1:T(8,128)}, u32[]{:S(2)}) copy-start(f32[128,16]{0,1:T(8,128)} %param.9) | copy-start | bytes 24580
  135.5 6.9 %copy-start.3 = (s32[4]{0:T(128)S(1)}, s32[4]{0:T(128)}, u32[]{:S(2)}) copy-start(s32[4]{0:T(128)} %param.10) | copy-start | bytes 52
  135.5 7.1 %copy-start = (f32[128,128]{1,0:T(8,128)S(1)}, f32[128,128]{1,0:T(8,128)}, u32[]{:S(2)}) copy-start(f32[128,128]{1,0:T(8,128)} %all-reduce.2.cloned.1.call-done) | copy-start | bytes 196612
  138.1 27.9 %all-to-all-start = ((bf16[4,16,5,3072]{3,1,2,0:T(8,128)(2,1)}), bf16[4,16,5,3072]{3,1,2,0:T(8,128)(2,1)S(1)}, u32[]{:S(2)}, u32[]{:S(2)}) async-start(bf16[4,16,5,3072]{3,1,2,0:T(8,128)(2,1)} %copy.39), calls=%async_computation | async-start | bytes 3932160 | tf_op jit(solution)/shard_map/all_to_all | solution.py:47
Sparse Core Ops, SparseCore 0:
  12.5 88.1 all-reduce.1
where the time goes:
time: 175 us; the launch traced here: 174 us
  waiting for transfers between devices  104 us (59%)
  other arithmetic  22.1 us (13%)
  local copies, waits for them, and re-layouts  16.3 us (9%)
  between operations  14.2 us (8%)
  matrix products  13.6 us (8%)
  starting transfers between devices  3.64 us (2%)
    psum x1, waiting for transfers between devices, local(): gram = lax.psum(partial_value, ('space', 'clus')) / total_rows  82 us
    all_to_all x1, waiting for transfers between devices, local(): lax.all_to_all(packed, 'clus', split_axis=0, concat_axis=3, tiled=True)  22.4 us
    another operation x7, other arithmetic, subspace(): lower = jnp.linalg.cholesky(inner)  12 us
    another operation x5, other arithmetic, subspace(): lax.linalg.triangular_solve(lower, image, left_side=False, lower=True, tr...  9.99 us
    reshape x2, local copies, waits for them, and re-layouts, local(): modes_full.astype(jnp.bfloat16)  7.12 us
    unnamed x9, local copies, waits for them, and re-layouts  6.29 us
    dot_general x1, matrix products, local(): lax.dot_general(flat, flat, (((1,), (1,)), ((), ())), preferred_element_t...  5.13 us
    dot_general x1, matrix products, local(): modes_full = jnp.dot(left, flat, preferred_element_type=jnp.float32)  4.86 us
  transfers between devices with their start and end apart: 2, of which 2 were waited for; matrix products, arithmetic and copies ran while one was open for 5% of the time, Pallas kernels for 0%

commit v1 on v0

--- a/solution.py
+++ b/solution.py
@@ -44,7 +44,10 @@
     left = jnp.transpose(rounded, (0, 2, 1)).reshape(clusters * mode_count, count)
     modes_full = jnp.dot(left, flat, preferred_element_type=jnp.float32)
     packed = modes_full.astype(jnp.bfloat16).reshape(clusters, mode_count, variables, cells)
-    modes_out = lax.all_to_all(packed, "clus", split_axis=0, concat_axis=3, tiled=True)
+    modes_out = jnp.concatenate(
+        lax.all_to_all(jnp.stack(jnp.split(packed, lax.axis_size("clus"), axis=0)), "clus", 0, 0),
+        axis=3,
+    )
     select = (successor[:, None] == cluster_ids[None, :]).astype(jnp.float32)
     wide = rounded.astype(jnp.float32)
     partner = jnp.einsum("ab,bsn->asn", select, wide, precision=lax.Precision.HIGHEST)

time: 175 us -> 175 us (level)
    another operation x0 -> x5, local copies, waits for them, and re-layouts: none -> 6.82 us  [local(): jnp.stack(jnp.split(packed, lax.axis_size('clus'), axis=0))]
    reshape x2 -> x1, local copies, waits for them, and re-layouts: 7.12 us -> 1.45 us  [local(): jnp.concatenate(lax.all_to_all(jnp.stack(jnp.split(packed, lax.axis_size(...]
where the time goes in v1:
time: 175 us
  waiting for transfers between devices  104 us (59%)
  other arithmetic  22.9 us (13%)
  local copies, waits for them, and re-layouts  16.9 us (10%)
  between operations  14.2 us (8%)
  matrix products  12.4 us (7%)
  starting transfers between devices  3.77 us (2%)
    psum x1, waiting for transfers between devices, local(): gram = lax.psum(partial_value, ('space', 'clus')) / total_rows  82 us
    all_to_all x1, waiting for transfers between devices, local(): lax.all_to_all(jnp.stack(jnp.split(packed, lax.axis_size('clus'), axis=0)...  22.4 us
    another operation x7, other arithmetic, subspace(): lower = jnp.linalg.cholesky(inner)  12 us
    another operation x5, other arithmetic, subspace(): lax.linalg.triangular_solve(lower, image, left_side=False, lower=True, tr...  9.99 us
    another operation x5, local copies, waits for them, and re-layouts, local(): jnp.stack(jnp.split(packed, lax.axis_size('clus'), axis=0))  6.82 us
    unnamed x9, local copies, waits for them, and re-layouts  6.28 us
    dot_general x1, matrix products, local(): lax.dot_general(flat, flat, (((1,), (1,)), ((), ())), preferred_element_t...  5.13 us
    all_to_all x1, starting transfers between devices, local(): lax.all_to_all(jnp.stack(jnp.split(packed, lax.axis_size('clus'), axis=0)...  3.73 us
  transfers between devices with their start and end apart: 2, of which 2 were waited for; matrix products, arithmetic and copies ran while one was open for 5% of the time, Pallas kernels for 0%

profile of v1, /device:TPU:8, one launch (start us, length us, event | category | flops | bytes accessed | tf_op | source)
XLA Modules:
  0.0 174.6 jit_solution(11020978703822970467)
XLA Ops:
  7.2 5.1 %convolution_bitcast_fusion = f32[128,128]{1,0:T(8,128)} fusion(bf16[128,5,3072]{2,0,1:T(8,128)(2,1)} %param.7), kind=kOutput, calls=%fused_computation.2 | convolution fusion | flops 503316480 | bytes 3997696 | tf_op jit(solution)/shard_map/dot_general | solution.py:31
  12.4 6.3 %copy.38 = bf16[128,5,3072]{0,2,1:T(8,128)(2,1)} copy(bf16[128,5,3072]{2,0,1:T(8,128)(2,1)} %param.7) | data formatting | bytes 7864320 | tf_op args[0]
  18.7 82.0 %all-reduce.2.cloned.1.call-done = f32[128,128]{1,0:T(8,128)} async-done(((f32[128,128]{1,0:T(8,128)}), f32[128,128]{1,0:T(8,128)}) %all-reduce.2.cloned.1.call-update) | async-done | bytes 65552 | tf_op jit(solution)/shard_map/psum | solution.py:34
  100.7 1.1 fusion.3
  102.1 5.9 %custom-call.8 = f32[4,16,16]{2,1,0:T(8,128)S(1)} custom-call(f32[4,16,16]{2,1,0:T(8,128)S(1)} %fusion.16), custom_call_target="Cholesky" | custom-call | tf_op jit(solution)/shard_map/jit(cholesky)/cholesky | solution.py:18
  108.2 4.9 %custom-call.9 = f32[4,1,16,16]{2,3,1,0:T(8,128)S(1)} custom-call(f32[4,1,16,16]{3,2,1,0:T(8,128)S(1)} %select_bitcast_fusion.1), custom_call_target="InvertDiagBlocksLowerTriangular" | custom-call | tf_op jit(solution)/shard_map/triangular_solve/custom-call.0 | solution.py:19
  113.1 0.3 convolution_bitcast_fusion.1
  113.4 1.1 fusion.1
  114.7 5.9 %custom-call.10 = f32[4,16,16]{2,1,0:T(8,128)S(1)} custom-call(f32[4,16,16]{2,1,0:T(8,128)S(1)} %fusion.14), custom_call_target="Cholesky" | custom-call | tf_op jit(solution)/shard_map/jit(cholesky)/cholesky | solution.py:18
  120.8 4.9 %custom-call.11 = f32[4,1,16,16]{2,3,1,0:T(8,128)S(1)} custom-call(f32[4,1,16,16]{3,2,1,0:T(8,128)S(1)} %select_bitcast_fusion), custom_call_target="InvertDiagBlocksLowerTriangular" | custom-call | tf_op jit(solution)/shard_map/triangular_solve/custom-call.0 | solution.py:19
  125.7 0.3 bitcast_convert_fusion
  126.0 3.6 %convolution_convert_fusion = bf16[64,15360]{1,0:T(8,128)(2,1)S(1)} fusion(bf16[64,128]{1,0:T(8,128)(2,1)S(1)} %bitcast.76, bf16[128,15360]{0,1:T(8,128)(2,1)} %bitcast.73), kind=kOutput, calls=%fused_computation | convolution fusion | flops 252641280 | bytes 5914624 | tf_op jit(solution)/shard_map/dot_general | solution.py:45
  129.6 0.9 fusion.35
  130.5 0.8 stack.15
  131.4 0.8 stack.18
  132.2 0.8 stack.17
  133.0 1.8 %stack.16 = bf16[1,1,16,5,3072]{4,3,2,1,0:T(8,128)(2,1)S(1)} reshape(bf16[16,15360]{1,0:T(8,128)(2,1)} %get-tuple-element.8) | data formatting | bytes 983040 | tf_op jit(solution)/shard_map/stack | solution.py:48
  134.8 0.9 pad_maximum_fusion
  135.7 2.6 %copy.39 = bf16[4,1,16,5,3072]{4,2,3,1,0:T(8,128)(2,1)} copy(bf16[4,1,16,5,3072]{4,3,2,1,0:T(8,128)(2,1)S(1)} %pad_maximum_fusion) | data formatting | bytes 3932160 | tf_op jit(solution)/shard_map/stack | solution.py:48
  138.3 3.7 %all-to-all-start = ((bf16[4,1,16,5,3072]{4,2,3,1,0:T(8,128)(2,1)}), bf16[4,1,16,5,3072]{4,2,3,1,0:T(8,128)(2,1)S(1)}, u32[]{:S(2)}, u32[]{:S(2)}) async-start(bf16[4,1,16,5,3072]{4,2,3,1,0:T(8,128)(2,1)} %copy.39), calls=%async_computation | async-start | bytes 3932160 | tf_op jit(solution)/shard_map/all_to_all | solution.py:48
  142.0 0.7 constant_dynamic-slice_fusion.1
  143.3 0.6 constant_dynamic-slice_fusion
  143.9 22.4 %all-to-all-done = bf16[4,1,16,5,3072]{4,2,3,1,0:T(8,128)(2,1)S(1)} async-done(((bf16[4,1,16,5,3072]{4,2,3,1,0:T(8,128)(2,1)}), bf16[4,1,16,5,3072]{4,2,3,1,0:T(8,128)(2,1)S(1)}, u32[]{:S(2)}, u32[]{:S(2)}) %all-to-all-start) | async-done | bytes 1966112 | tf_op jit(solution)/shard_map/all_to_all | solution.py:48
  166.3 1.4 copy.52
  (29 shorter events, 1.6 us)
Async XLA Ops:
  7.2 5.2 %copy-start.2 = (s32[128]{0:T(128)S(1)}, s32[128]{0:T(128)}, u32[]{:S(2)}) copy-start(s32[128]{0:T(128)} %param.8) | copy-start | bytes 1540
  7.2 93.5 %all-reduce.2.cloned.1.call-start = ((), (), s32[]{:S(2)}) async-start(), calls=%async_computation.1 | async-start | bytes 131072 | tf_op jit(solution)/shard_map/psum | solution.py:34
  12.4 88.3 %copy-start.1 = (f32[128,16]{0,1:T(8,128)S(1)}, f32[128,16]{0,1:T(8,128)}, u32[]{:S(2)}) copy-start(f32[128,16]{0,1:T(8,128)} %param.9) | copy-start | bytes 24580
  138.3 4.4 %copy-start.3 = (s32[4]{0:T(128)S(1)}, s32[4]{0:T(128)}, u32[]{:S(2)}) copy-start(s32[4]{0:T(128)} %param.10) | copy-start | bytes 52
  138.3 4.6 %copy-start = (f32[128,128]{1,0:T(8,128)S(1)}, f32[128,128]{1,0:T(8,128)}, u32[]{:S(2)}) copy-start(f32[128,128]{1,0:T(8,128)} %all-reduce.2.cloned.1.call-done) | copy-start | bytes 196612
  138.3 28.0 %all-to-all-start = ((bf16[4,1,16,5,3072]{4,2,3,1,0:T(8,128)(2,1)}), bf16[4,1,16,5,3072]{4,2,3,1,0:T(8,128)(2,1)S(1)}, u32[]{:S(2)}, u32[]{:S(2)}) async-start(bf16[4,1,16,5,3072]{4,2,3,1,0:T(8,128)(2,1)} %copy.39), calls=%async_computation | async-start | bytes 3932160 | tf_op jit(solution)/shard_map/all_to_all | solution.py:48
Sparse Core Ops, SparseCore 0:
  12.5 88.1 all-reduce.1
